TPU v7x, 32 devices: a whole 2x2x4 slice. The times are simulated.
32 devices in a mesh: epoch: 4 (over y, x), strip: 8 (over z, core).
Axes of the slice: x: 2, y: 2, z: 4, core: 2. Of those that a mesh axis runs over, the one named last changes fastest.
Arguments:
- raw_tiles: float32 [4, 96, 256, 512], P('epoch', 'strip'), may hold values from -6 to 6
- tile_kind: int32 [4, 96], P('epoch', 'strip'), may hold values from 0 to 3
- tile_invvar: float32 [4, 96], P('epoch', 'strip'), may hold values from 0.2 to 5
- tile_heights: int32 [4, 8, 12], P('epoch'), may hold values from 1 to 256, 2048 in all within a row
- row_interp: float32 [4, 256, 256], replicated, may hold values from -0.4 to 1.9
- col_interp: float32 [4, 512, 512], replicated, may hold values from -0.4 to 1.9
- psf_profiles: float32 [2, 2, 31], replicated, may hold values from -1 to 1
- psf_poly: float32 [4, 2, 6], replicated, may hold values from -1 to 1
Outputs:
- difference: float32 [4, 2048, 4096], P('epoch', 'strip')
Inputs may be any that keep to these rules, and one draw needn't show every extreme that they name: `tile_heights`: along the last dimension, the heights of one column block's tiles from the top of the patch down; they sum to 2048, and the tallest is exactly 256.
All inputs are finite; a program needn't handle non-finite values.
Results may differ from a plain program's by a relative error of at most 0.0003.
Values sent between devices are 32-bit elements; how exact they have to be, the bound alone decides.
No kernel may reach another device: no remote copies, remote signals or barrier semaphores. Data moves between devices by JAX's collectives and lax.ppermute only.
A program may use at most 128 MiB of HBM per device.

v0:
```python
import jax
import jax.numpy as jnp
from jax import lax
from jax.sharding import PartitionSpec as P

ROWS_DEV = 256
KSIZE = 31
precise = lax.Precision.HIGHEST


def padded_2(value, sides, width):
    for axis, dim in sides:
        count, length = (lax.axis_size(axis), value.shape[dim])
        up = [(i, (i + 1) % count) for i in range(count - 1)]
        down = [(j, i) for i, j in up]
        last = lax.slice_in_dim(value, length - width, length, axis=dim)
        initial = lax.slice_in_dim(value, 0, width, axis=dim)
        before = lax.ppermute(last, axis, up)
        after = lax.ppermute(initial, axis, down)
        value = jnp.concatenate([before, value, after], axis=dim)
    return value


def positions(first_cell, length, extent):
    counter = (first_cell + jnp.arange(length)).astype(jnp.float32)
    return (2.0 * counter + 1.0) / extent - 1.0


def coeff_maps(poly_rows, row_coords, col_coords):
    row_term = row_coords[:, None]
    col_term = col_coords[None, :]
    terms = poly_rows[..., None, None]
    return (
        terms[..., 0, :, :]
        + terms[..., 1, :, :] * row_term
        + terms[..., 2, :, :] * col_term
        + terms[..., 3, :, :] * row_term * row_term
        + terms[..., 4, :, :] * row_term * col_term
        + terms[..., 5, :, :] * col_term * col_term
    )


def row_pass(padded, profiles):
    margin = KSIZE // 2
    rows_out = padded.shape[0] - 2 * margin
    offset = jnp.arange(padded.shape[0])[None, :] - jnp.arange(rows_out)[:, None]
    onehot = (offset[:, :, None] == jnp.arange(KSIZE)[None, None, :]).astype(jnp.float32)
    banded = jnp.einsum("rqi,ki->krq", onehot, profiles[:, 0, :], precision=precise)
    return jnp.einsum("krq,qc->krc", banded, padded, precision=precise)


def col_pass(padded, profiles):
    margin = KSIZE // 2
    basis_count, rows_out, wide_in = padded.shape
    width_out = wide_in - 2 * margin
    block_cols = 128
    block_count = width_out // block_cols
    extended = jnp.pad(padded, ((0, 0), (0, 0), (0, block_cols - 2 * margin)))
    leading = extended[:, :, :width_out].reshape(basis_count, rows_out, block_count, block_cols)
    trailing = extended[:, :, block_cols : block_cols + width_out].reshape(
        basis_count, rows_out, block_count, block_cols
    )
    window = jnp.concatenate([leading, trailing[:, :, :, : 2 * margin]], axis=3)
    offset = jnp.arange(block_cols + 2 * margin)[:, None] - jnp.arange(block_cols)[None, :]
    onehot = (offset[:, :, None] == jnp.arange(KSIZE)[None, None, :]).astype(jnp.float32)
    toeplitz = jnp.einsum("mci,ki->kmc", onehot, profiles[:, 1, :], precision=precise)
    result = jnp.einsum("krnm,kmc->krnc", window, toeplitz, precision=precise)
    return result.reshape(basis_count, rows_out, width_out)


def shards(
    raw_tiles, tile_kind, tile_invvar, tile_heights, row_interp, col_interp, psf_profiles, psf_poly
):
    strips = lax.axis_size("strip")
    strip_index = lax.axis_index("strip")
    tiles_dev = raw_tiles.shape[1]
    tile_rows = raw_tiles.shape[2]
    tile_cols = raw_tiles.shape[3]
    blocks = tile_heights.shape[1]
    per_col = tile_heights.shape[2]
    ncol_all = blocks * tile_cols
    nrow_all = ROWS_DEV * strips
    sources = strips // blocks
    first_tile = strip_index * tiles_dev
    block_index = first_tile // per_col
    column_heights = lax.dynamic_index_in_dim(tile_heights[0], block_index, 0, keepdims=False)
    column_starts = jnp.cumsum(column_heights) - column_heights
    offset_in = first_tile % per_col
    my_heights = lax.dynamic_slice_in_dim(column_heights, offset_in, tiles_dev)
    my_starts = lax.dynamic_slice_in_dim(column_starts, offset_in, tiles_dev)
    live_rows = jnp.arange(tile_rows)[None, :] < my_heights[:, None]
    masked = jnp.where(live_rows[:, :, None], raw_tiles[0], 0.0)
    tile_kinds = tile_kind[0]
    half_warped = jnp.einsum(
        "tij,tjk->tik", jnp.take(row_interp, tile_kinds, axis=0), masked, precision=precise
    )
    warped = jnp.einsum(
        "tik,tlk->til", half_warped, jnp.take(col_interp, tile_kinds, axis=0), precision=precise
    )
    sky_rows = jnp.arange(nrow_all)
    covering = jnp.sum((sky_rows[:, None] >= my_starts[None, :]).astype(jnp.int32), axis=1) - 1
    chosen = jnp.maximum(covering, 0)
    member = chosen[:, None] == jnp.arange(tiles_dev)[None, :]
    start_of = jnp.sum(jnp.where(member, my_starts[None, :], 0), axis=1)
    height_of = jnp.sum(jnp.where(member, my_heights[None, :], 0), axis=1)
    weight_of = jnp.sum(jnp.where(member, tile_invvar[0][None, :], 0.0), axis=1)
    local_row = sky_rows - start_of
    covered = (covering >= 0) & (local_row < height_of)
    source = chosen * tile_rows + jnp.clip(local_row, 0, tile_rows - 1)
    picked = jnp.take(warped.reshape(tiles_dev * tile_rows, tile_cols), source, axis=0)
    outgoing = jnp.where(covered[:, None], picked, 0.0).reshape(strips, ROWS_DEV, tile_cols)
    out_weight = jnp.where(covered, weight_of, 0.0).reshape(strips, ROWS_DEV)
    incoming, in_weight = (
        lax.all_to_all(outgoing, "strip", split_axis=0, concat_axis=0, tiled=True),
        lax.all_to_all(out_weight, "strip", split_axis=0, concat_axis=0, tiled=True),
    )
    gathered = jnp.sum(incoming.reshape(blocks, sources, ROWS_DEV, tile_cols), axis=1)
    weights = jnp.transpose(jnp.sum(in_weight.reshape(blocks, sources, ROWS_DEV), axis=1))
    science_blocks = jnp.transpose(gathered, (1, 0, 2))
    weighted = (science_blocks * weights[:, :, None]).reshape(ROWS_DEV, ncol_all)
    science = science_blocks.reshape(ROWS_DEV, ncol_all)
    row_coords = positions(strip_index * ROWS_DEV, ROWS_DEV, nrow_all)
    epochs = lax.axis_size("epoch")
    share_cols = ncol_all // epochs
    weighted_sum, weight_sum = (
        lax.psum_scatter(weighted, "epoch", scatter_dimension=1, tiled=True),
        lax.psum_scatter(weights, "epoch", scatter_dimension=1, tiled=True),
    )
    template = (
        weighted_sum.reshape(ROWS_DEV, blocks // epochs, tile_cols) / weight_sum[:, :, None]
    ).reshape(ROWS_DEV, share_cols)
    padded = padded_2(template, (("epoch", 1), ("strip", 0)), KSIZE // 2)
    convolved = col_pass(row_pass(padded, psf_profiles), psf_profiles)
    col_coords = positions(lax.axis_index("epoch") * share_cols, share_cols, ncol_all)
    coeffs = coeff_maps(psf_poly, row_coords, col_coords)
    matched = coeffs[:, 0] * convolved[0][None] + coeffs[:, 1] * convolved[1][None]
    returned = lax.all_to_all(matched, "epoch", split_axis=0, concat_axis=2, tiled=True)
    return science[None] - returned


def solution(mesh):
    in_specs = (
        P("epoch", "strip", None, None),
        P("epoch", "strip"),
        P("epoch", "strip"),
        P("epoch", None, None),
        P(),
        P(),
        P(),
        P(),
    )
    out_specs = P("epoch", "strip", None)
    return jax.shard_map(shards, mesh=mesh, in_specs=in_specs, out_specs=out_specs, check_vma=False)
```

profile of v0, /device:TPU:9, one launch (start us, length us, event | category | flops | bytes accessed | tf_op | source)
XLA Modules:
  0.0 344.2 jit_solution(10702041812588887044)
XLA Ops:
  6.5 0.8 fusion.34
  7.3 0.2 reduce-window.8
  7.5 0.7 bitcast_subtract_fusion.1
  8.2 0.1 convert_reduce_fusion
  8.3 0.1 select_reduce_fusion.1
  8.5 0.8 select_reduce_fusion
  9.3 0.6 copy.67
  9.9 5.6 %all-to-all-start.1 = ((f32[8,1,256]{2,1,0:T(1,128)}), f32[8,1,256]{2,1,0:T(1,128)S(1)}, u32[]{:S(2)}, u32[]{:S(2)}) async-start(f32[8,1,256]{2,1,0:T(1,128)} %copy.67), calls=%async_computation.1 | async-start | bytes 16384 | tf_op jit(solution)/shard_map/all_to_all | solution.py:115
  15.5 0.1 iota_compare_fusion.10
  15.6 0.7 fusion.32
  16.2 0.7 compare_and_fusion.2
  17.0 2.4 gather_fusion
  19.4 8.8 %gather_fusion.1 = f32[12,512,512]{2,1,0:T(8,128)} fusion(f32[4,512,512]{2,1,0:T(8,128)} %param.13, s32[1024]{0:T(1024)S(1)} %pad_clamp_fusion), kind=kCustom, calls=%fused_computation.1 | custom fusion | bytes 25165872 | tf_op jit(solution)/shard_map/jit(_take)/gather | solution.py:98
  28.2 8.8 %fusion.3 = f32[12,256,512]{2,1,0:T(8,128)S(1)} fusion(f32[1,12,256,512]{3,2,1,0:T(8,128)} %param.8, f32[12,256,256]{2,1,0:T(8,128)} %gather_fusion, pred[12,256]{1,0:T(8,128)(4,1)S(1)} %iota_compare_fusion.10, pred[12]{0:T(512)(128)(4,1)S(1)} %compare_and_fusion.2), kind=kOutput, calls=%fused_computation.9 | convolution fusion | flops 4834197504 | bytes 15731724 | tf_op jit(solution)/shard_map/tij,tjk->tik/dot_general | solution.py:94
  37.0 15.8 %fusion = f32[12,256,512]{2,1,0:T(8,128)} fusion(f32[12,256,512]{2,1,0:T(8,128)S(1)} %fusion.3, f32[12,512,512]{2,1,0:T(8,128)} %gather_fusion.1, pred[12]{0:T(512)(128)(4,1)S(1)} %compare_and_fusion.2), kind=kOutput, calls=%fused_computation.4 | convolution fusion | flops 9666822144 | bytes 25165836 | tf_op jit(solution)/shard_map/tik,tlk->til/dot_general | solution.py:97
  52.8 12.3 %gather_fusion.2 = f32[2048,512]{1,0:T(8,128)} fusion(f32[3072,512]{1,0:T(8,128)} %bitcast.83, s32[2048]{0:T(1024)S(1)} %broadcast_clamp_fusion), kind=kCustom, calls=%fused_computation.2 | custom fusion | bytes 8396800 | tf_op jit(solution)/shard_map/jit(_take)/gather | solution.py:110
  65.1 4.0 %select_select_fusion = f32[8,256,512]{2,1,0:T(8,128)} fusion(f32[8,256,512]{2,1,0:T(8,128)} %bitcast.86, pred[8,256]{1,0:T(8,128)(4,1)S(1)} %get-tuple-element.18, pred[8,256]{1,0:T(8,128)(4,1)S(1)} %get-tuple-element.17), kind=kLoop, calls=%fused_computation.20 | loop fusion | flops 2097152 | bytes 8392704 | tf_op jit(solution)/shard_map/jit(_where)/select_n | solution.py:111
  69.1 0.0 all-to-all-done.1
  69.1 5.1 %all-to-all-start = ((f32[8,256,512]{2,1,0:T(8,128)}), f32[8,256,512]{2,1,0:T(8,128)}, u32[]{:S(2)}, u32[]{:S(2)}) async-start(f32[8,256,512]{2,1,0:T(8,128)} %select_select_fusion), calls=%async_computation | async-start | bytes 8388608 | tf_op jit(solution)/shard_map/all_to_all | solution.py:114
  74.2 90.5 %all-to-all-done = f32[8,256,512]{2,1,0:T(8,128)} async-done(((f32[8,256,512]{2,1,0:T(8,128)}), f32[8,256,512]{2,1,0:T(8,128)}, u32[]{:S(2)}, u32[]{:S(2)}) %all-to-all-start) | async-done | bytes 4194336 | tf_op jit(solution)/shard_map/all_to_all | solution.py:114
  164.7 5.3 %copy.60 = f32[8,256,512]{1,2,0:T(8,128)} copy(f32[8,256,512]{2,1,0:T(8,128)} %all-to-all-done) | data formatting | bytes 8388608 | tf_op jit(solution)/shard_map/all_to_all | solution.py:114
  170.0 4.6 %bitcast_multiply_fusion = f32[256,8,512]{0,2,1:T(8,128)} fusion(f32[8,256,512]{1,2,0:T(8,128)} %copy.60, f32[256,8]{0,1:T(8,128)S(1)} %bitcast.96), kind=kLoop, calls=%fused_computation.19 | loop fusion | flops 1048576 | bytes 8396800 | tf_op jit(solution)/shard_map/mul | solution.py:120
  174.6 5.6 %copy.77 = f32[256,4096]{1,0:T(8,128)} copy(f32[256,4096]{0,1:T(8,128)} %bitcast.87) | data formatting | bytes 8388608 | tf_op jit(solution)/shard_map/reshape | solution.py:120
  180.2 0.0 reduce-scatter.2.cloned.1.call-update
  180.2 0.6 copy-done.2
  180.9 0.1 fusion.45
  181.0 0.1 copy.61
  181.1 0.1 copy.62
  181.2 0.1 copy.64
  181.3 0.1 copy.65
  181.4 0.1 copy.63
  181.5 0.1 copy.66
  181.6 0.6 dynamic-slice.1
  182.8 0.1 multiply_add_fusion
  182.9 0.1 broadcast_multiply_fusion
  183.0 4.8 %fusion.25 = f32[2,256,286]{2,0,1:T(2,128)S(1)} fusion(f32[2,31,1]{1,0,2:T(2,128)S(1)} %bitcast.107, s32[256,286]{1,0:T(8,128)S(1)} %iota_subtract_fusion), kind=kOutput, calls=%fused_computation.39 | convolution fusion | flops 56742400 | bytes 878840 | tf_op jit(solution)/shard_map/rqi,ki->krq/dot_general | solution.py:48
  187.8 4.2 %add_add_fusion = f32[4,2,256,1024]{3,2,0,1:T(8,128)} fusion(f32[4,2,1024]{2,0,1:T(4,128)S(1)} %get-tuple-element.28, f32[1024]{0:T(1024)S(1)} %multiply_add_fusion.1, f32[4,2,256]{2,0,1:T(4,128)S(1)} %get-tuple-element.32, f32[4,2,256]{2,0,1:T(4,128)S(1)} %get-tuple-element.33, f32[4,2,1024]{2,0,1:T(4,128)S(1)} %get-tuple-element.27, ...), kind=kLoop, calls=%fused_computation.7 | loop fusion | flops 10485760 | bytes 8482816 | tf_op jit(solution)/shard_map/add | solution.py:34
  192.0 8.9 %all-reduce.1 = f32[256,8]{0,1:T(8,128)S(1)} all-reduce(f32[256,8]{0,1:T(8,128)S(1)} %bitcast.97), channel_id=3, replica_groups=mesh['epoch'=4,'strip'=8] {'epoch'}, use_global_device_ids=true, to_apply=%region_6.7.clone | all-reduce | flops 2048 | bytes 16384
  200.9 0.1 copy.69
  201.1 0.3 div.32
  201.4 0.2 copy.81
  201.6 33.4 %reduce-scatter.2.cloned.1.call-done = f32[256,1024]{1,0:T(8,128)} async-done(((f32[256,4096]{1,0:T(8,128)}), f32[256,1024]{1,0:T(8,128)}) %reduce-scatter.2.cloned.1.call-update) | async-done | bytes 1048592 | tf_op jit(solution)/shard_map/reduce_scatter | solution.py:126
  235.1 1.4 div.34
  236.5 0.1 fusion.44
  236.6 3.1 collective-permute-start
  239.7 1.3 collective-permute-start.1
  241.0 0.6 collective-permute-done
  241.6 5.1 %collective-permute-done.1 = f32[256,15]{1,0:T(8,128)S(1)} collective-permute-done((f32[256,15]{1,0:T(8,128)S(1)}, f32[256,15]{1,0:T(8,128)S(1)}, u32[]{:S(2)}, u32[]{:S(2)}) %collective-permute-start.1) | collective-permute-done | bytes 15392 | tf_op jit(solution)/shard_map/ppermute | solution.py:19
  246.7 0.8 concatenate.9
  247.5 4.4 %collective-permute-start.2 = (f32[15,1054]{1,0:T(8,128)S(1)}, f32[15,1054]{1,0:T(8,128)S(1)}, u32[]{:S(2)}, u32[]{:S(2)}) collective-permute-start(f32[15,1054]{1,0:T(8,128)S(1)} %get-tuple-element.13), channel_id=1, source_target_pairs={{0,1},{1,2},{2,3},{3,4},{4,5},{5,6},{6,7},{8,9},{9,10},{10,11},{11... | collective-permute-start | bytes 189728 | tf_op jit(solution)/shard_map/ppermute | solution.py:18
  251.9 2.1 collective-permute-start.3
  254.1 1.0 fusion.27
  255.1 2.5 collective-permute-done.3
  257.6 3.7 %fusion.20 = f32[2,256,1054]{1,2,0:T(8,128)S(1)} fusion(f32[15,1054]{1,0:T(8,128)S(1)} %collective-permute-done.3, f32[256,1054]{1,0:T(8,128)S(1)} %concatenate.9, f32[15,1054]{1,0:T(8,128)S(1)} %collective-permute-done.2, f32[2,256,286]{2,0,1:T(2,128)S(1)} %fusion.25), kind=kOutput, calls=%fused_computation.34 | convolution fusion | flops 1852674816 | bytes 3950096 | tf_op jit(solution)/shard_map/krq,qc->krc/dot_general | solution.py:49
  261.3 0.3 fusion.41
  261.7 2.3 fusion.13
  264.0 0.1 fusion.42
  264.1 0.3 copy.72
  264.4 0.3 copy.73
  264.8 4.7 %fusion.8 = f32[4,256,1024]{2,1,0:T(8,128)S(1)} fusion(f32[4,2,256,1024]{3,2,0,1:T(8,128)} %add_add_fusion, f32[256,1024]{1,0:T(8,128)S(1)} %copy.73, f32[256,1024]{1,0:T(8,128)S(1)} %copy.72), kind=kLoop, calls=%fused_computation.15 | loop fusion | flops 3145728 | bytes 14680064 | tf_op jit(solution)/shard_map/add | solution.py:136
  269.5 50.8 %all_to_all.29 = f32[4,256,1024]{2,1,0:T(8,128)} all-to-all(f32[4,256,1024]{2,1,0:T(8,128)S(1)} %fusion.8), channel_id=1, replica_groups=mesh['epoch'=4,'strip'=8] {'epoch'}, dimensions={0} | all-to-all | bytes 8388608 | tf_op jit(solution)/shard_map/all_to_all | solution.py:137
  320.3 5.4 %copy.74 = f32[4,256,1024]{1,2,0:T(8,128)} copy(f32[4,256,1024]{2,1,0:T(8,128)} %all_to_all.29) | data formatting | bytes 8388608 | tf_op jit(solution)/shard_map/all_to_all | solution.py:137
  325.7 6.1 %bitcast_subtract_fusion = f32[1,256,4096]{1,2,0:T(8,128)} fusion(f32[1,256,4096]{1,2,0:T(8,128)} %bitcast.85, f32[1,256,4096]{1,2,0:T(8,128)} %bitcast.84), kind=kLoop, calls=%fused_computation.18 | loop fusion | flops 1048576 | bytes 12582912 | tf_op jit(solution)/shard_map/sub | solution.py:138
  331.8 5.6 %copy.75 = f32[1,256,4096]{2,1,0:T(8,128)} copy(f32[1,256,4096]{1,2,0:T(8,128)} %bitcast_subtract_fusion) | data formatting | bytes 8388608 | tf_op jit(solution)/shard_map/sub | solution.py:138
  (35 shorter events, 0.3 us)
Async XLA Ops:
  6.5 10.5 %copy-start = (f32[4,256,256]{2,1,0:T(8,128)S(1)}, f32[4,256,256]{2,1,0:T(8,128)}, u32[]{:S(2)}) copy-start(f32[4,256,256]{2,1,0:T(8,128)} %param.12) | copy-start | bytes 3145732
  9.9 59.2 %all-to-all-start.1 = ((f32[8,1,256]{2,1,0:T(1,128)}), f32[8,1,256]{2,1,0:T(1,128)S(1)}, u32[]{:S(2)}, u32[]{:S(2)}) async-start(f32[8,1,256]{2,1,0:T(1,128)} %copy.67), calls=%async_computation.1 | async-start | bytes 16384 | tf_op jit(solution)/shard_map/all_to_all | solution.py:115
  69.1 95.6 %all-to-all-start = ((f32[8,256,512]{2,1,0:T(8,128)}), f32[8,256,512]{2,1,0:T(8,128)}, u32[]{:S(2)}, u32[]{:S(2)}) async-start(f32[8,256,512]{2,1,0:T(8,128)} %select_select_fusion), calls=%async_computation | async-start | bytes 8388608 | tf_op jit(solution)/shard_map/all_to_all | solution.py:114
  74.2 160.9 %reduce-scatter.2.cloned.1.call-start = ((), (), s32[]{:S(2)}) async-start(), calls=%async_computation.4 | async-start | bytes 5242880 | tf_op jit(solution)/shard_map/reduce_scatter | solution.py:126
  180.2 0.7 copy-start.2
  180.2 1.4 copy-start.4
  180.2 2.6 copy-start.3
  236.6 5.0 %collective-permute-start = (f32[256,15]{1,0:T(8,128)S(1)}, f32[256,15]{1,0:T(8,128)S(1)}, u32[]{:S(2)}, u32[]{:S(2)}) collective-permute-start(f32[256,15]{1,0:T(8,128)S(1)} %get-tuple-element.16), channel_id=1, source_target_pairs={{0,8},{8,16},{16,24},{1,9},{9,17},{17,25},{2,10},{10,18},{18,26},{... | collective-permute-start | bytes 46088 | tf_op jit(solution)/shard_map/ppermute | solution.py:18
  239.7 7.0 %collective-permute-start.1 = (f32[256,15]{1,0:T(8,128)S(1)}, f32[256,15]{1,0:T(8,128)S(1)}, u32[]{:S(2)}, u32[]{:S(2)}) collective-permute-start(f32[256,15]{1,0:T(8,128)S(1)} %get-tuple-element.15), channel_id=1, source_target_pairs={{8,0},{16,8},{24,16},{9,1},{17,9},{25,17},{10,2},{18,10},{26,18},{... | collective-permute-start | bytes 46088 | tf_op jit(solution)/shard_map/ppermute | solution.py:19
  247.5 7.5 %collective-permute-start.2 = (f32[15,1054]{1,0:T(8,128)S(1)}, f32[15,1054]{1,0:T(8,128)S(1)}, u32[]{:S(2)}, u32[]{:S(2)}) collective-permute-start(f32[15,1054]{1,0:T(8,128)S(1)} %get-tuple-element.13), channel_id=1, source_target_pairs={{0,1},{1,2},{2,3},{3,4},{4,5},{5,6},{6,7},{8,9},{9,10},{10,11},{11... | collective-permute-start | bytes 189728 | tf_op jit(solution)/shard_map/ppermute | solution.py:18
  251.9 5.7 %collective-permute-start.3 = (f32[15,1054]{1,0:T(8,128)S(1)}, f32[15,1054]{1,0:T(8,128)S(1)}, u32[]{:S(2)}, u32[]{:S(2)}) collective-permute-start(f32[15,1054]{1,0:T(8,128)S(1)} %get-tuple-element.14), channel_id=1, source_target_pairs={{1,0},{2,1},{3,2},{4,3},{5,4},{6,5},{7,6},{9,8},{10,9},{11,10},{12... | collective-permute-start | bytes 189728 | tf_op jit(solution)/shard_map/ppermute | solution.py:19
  325.7 11.7 %copy-start.1 = (f32[4,256,256]{2,1,0:T(8,128)S(1)}, f32[4,256,256]{2,1,0:T(8,128)}, u32[]{:S(2)}) copy-start(f32[4,256,256]{2,1,0:T(8,128)} %param.12) | copy-start | bytes 3145732
Sparse Core Ops, SparseCore 0:
  180.4 54.6 reduce-scatter.1
where the time goes:
time: 345 us; the launch traced here: 344 us
  waiting for transfers between devices  132 us (38%)
  blocking collectives  59.7 us (17%)
  local copies, waits for them, and re-layouts  51.5 us (15%)
  matrix products  36.4 us (11%)
  other arithmetic  28.5 us (8%)
  starting transfers between devices  21.6 us (6%)
  between operations  14.3 us (4%)
    all_to_all x1, waiting for transfers between devices, shards(): lax.all_to_all(outgoing, 'strip', split_axis=0, concat_axis=0, tiled=True)  90.5 us
    all_to_all x1, blocking collectives, shards(): lax.all_to_all(matched, 'epoch', split_axis=0, concat_axis=2, tiled=True)  50.8 us
    reduce_scatter x1, waiting for transfers between devices, shards(): lax.psum_scatter(weighted, 'epoch', scatter_dimension=1, tiled=True)  33.4 us
    dot_general x1, matrix products, shards(): jnp.einsum('tik,tlk->til', half_warped, jnp.take(col_interp, tile_kinds,...  15.8 us
    gather x1, local copies, waits for them, and re-layouts, shards(): jnp.take(warped.reshape(tiles_dev * tile_rows, tile_cols), source, axis=0)  12.3 us
    unnamed x1, blocking collectives  8.89 us
    gather x1, local copies, waits for them, and re-layouts, shards(): jnp.take(col_interp, tile_kinds, axis=0)  8.79 us
    dot_general x1, matrix products, shards(): jnp.einsum('tij,tjk->tik', jnp.take(row_interp, tile_kinds, axis=0), mask...  8.77 us
  transfers between devices with their start and end apart: 7, of which 5 were waited for; matrix products, arithmetic and copies ran while one was open for 19% of the time, Pallas kernels for 0%

commit v1 on v0

--- a/solution.py
+++ b/solution.py
@@ -134,7 +134,12 @@
     col_coords = positions(lax.axis_index("epoch") * share_cols, share_cols, ncol_all)
     coeffs = coeff_maps(psf_poly, row_coords, col_coords)
     matched = coeffs[:, 0] * convolved[0][None] + coeffs[:, 1] * convolved[1][None]
-    returned = lax.all_to_all(matched, "epoch", split_axis=0, concat_axis=2, tiled=True)
+    returned = jnp.concatenate(
+        lax.all_to_all(
+            jnp.stack(jnp.split(matched, lax.axis_size("epoch"), axis=0)), "epoch", 0, 0
+        ),
+        axis=2,
+    )
     return science[None] - returned
 
 

time: 345 us -> 346 us (level)
  no operation moved by 1% of the time
where the time goes in v1:
time: 346 us; the launch traced here: 345 us
  waiting for transfers between devices  132 us (38%)
  blocking collectives  59.7 us (17%)
  local copies, waits for them, and re-layouts  52.1 us (15%)
  matrix products  36.4 us (11%)
  other arithmetic  29 us (8%)
  starting transfers between devices  21.6 us (6%)
  between operations  14.5 us (4%)
    all_to_all x1, waiting for transfers between devices, shards(): lax.all_to_all(outgoing, 'strip', split_axis=0, concat_axis=0, tiled=True)  90.5 us
    all_to_all x1, blocking collectives, shards(): lax.all_to_all(jnp.stack(jnp.split(matched, lax.axis_size('epoch'), axis=...  50.8 us
    reduce_scatter x1, waiting for transfers between devices, shards(): lax.psum_scatter(weighted, 'epoch', scatter_dimension=1, tiled=True)  33.3 us
    dot_general x1, matrix products, shards(): jnp.einsum('tik,tlk->til', half_warped, jnp.take(col_interp, tile_kinds,...  15.8 us
    gather x1, local copies, waits for them, and re-layouts, shards(): jnp.take(warped.reshape(tiles_dev * tile_rows, tile_cols), source, axis=0)  12.3 us
    unnamed x1, blocking collectives  8.88 us
    gather x1, local copies, waits for them, and re-layouts, shards(): jnp.take(col_interp, tile_kinds, axis=0)  8.78 us
    dot_general x1, matrix products, shards(): jnp.einsum('tij,tjk->tik', jnp.take(row_interp, tile_kinds, axis=0), mask...  8.77 us
  transfers between devices with their start and end apart: 7, of which 5 were waited for; matrix products, arithmetic and copies ran while one was open for 19% of the time, Pallas kernels for 0%

profile of v1, /device:TPU:9, one launch (start us, length us, event | category | flops | bytes accessed | tf_op | source)
XLA Modules:
  0.0 345.2 jit_solution(6730000245482350128)
XLA Ops:
  6.5 0.8 fusion.34
  7.3 0.2 reduce-window.8
  7.5 0.7 bitcast_subtract_fusion.1
  8.2 0.1 convert_reduce_fusion
  8.3 0.1 select_reduce_fusion.1
  8.5 0.8 select_reduce_fusion
  9.3 0.6 copy.67
  9.9 5.6 %all-to-all-start.1 = ((f32[8,1,256]{2,1,0:T(1,128)}), f32[8,1,256]{2,1,0:T(1,128)S(1)}, u32[]{:S(2)}, u32[]{:S(2)}) async-start(f32[8,1,256]{2,1,0:T(1,128)} %copy.67), calls=%async_computation.1 | async-start | bytes 16384 | tf_op jit(solution)/shard_map/all_to_all | solution.py:115
  15.5 0.1 iota_compare_fusion.10
  15.6 0.7 fusion.32
  16.2 0.7 compare_and_fusion.2
  17.0 2.4 gather_fusion
  19.4 8.8 %gather_fusion.1 = f32[12,512,512]{2,1,0:T(8,128)} fusion(f32[4,512,512]{2,1,0:T(8,128)} %param.13, s32[1024]{0:T(1024)S(1)} %pad_clamp_fusion), kind=kCustom, calls=%fused_computation.1 | custom fusion | bytes 25165872 | tf_op jit(solution)/shard_map/jit(_take)/gather | solution.py:98
  28.2 8.8 %fusion.3 = f32[12,256,512]{2,1,0:T(8,128)S(1)} fusion(f32[1,12,256,512]{3,2,1,0:T(8,128)} %param.8, f32[12,256,256]{2,1,0:T(8,128)} %gather_fusion, pred[12,256]{1,0:T(8,128)(4,1)S(1)} %iota_compare_fusion.10, pred[12]{0:T(512)(128)(4,1)S(1)} %compare_and_fusion.2), kind=kOutput, calls=%fused_computation.9 | convolution fusion | flops 4834197504 | bytes 15731724 | tf_op jit(solution)/shard_map/tij,tjk->tik/dot_general | solution.py:94
  37.0 15.8 %fusion = f32[12,256,512]{2,1,0:T(8,128)} fusion(f32[12,256,512]{2,1,0:T(8,128)S(1)} %fusion.3, f32[12,512,512]{2,1,0:T(8,128)} %gather_fusion.1, pred[12]{0:T(512)(128)(4,1)S(1)} %compare_and_fusion.2), kind=kOutput, calls=%fused_computation.4 | convolution fusion | flops 9666822144 | bytes 25165836 | tf_op jit(solution)/shard_map/tik,tlk->til/dot_general | solution.py:97
  52.8 12.3 %gather_fusion.2 = f32[2048,512]{1,0:T(8,128)} fusion(f32[3072,512]{1,0:T(8,128)} %bitcast.88, s32[2048]{0:T(1024)S(1)} %broadcast_clamp_fusion), kind=kCustom, calls=%fused_computation.2 | custom fusion | bytes 8396800 | tf_op jit(solution)/shard_map/jit(_take)/gather | solution.py:110
  65.1 4.0 %select_select_fusion = f32[8,256,512]{2,1,0:T(8,128)} fusion(f32[8,256,512]{2,1,0:T(8,128)} %bitcast.90, pred[8,256]{1,0:T(8,128)(4,1)S(1)} %get-tuple-element.22, pred[8,256]{1,0:T(8,128)(4,1)S(1)} %get-tuple-element.21), kind=kLoop, calls=%fused_computation.21 | loop fusion | flops 2097152 | bytes 8392704 | tf_op jit(solution)/shard_map/jit(_where)/select_n | solution.py:111
  69.1 5.1 %all-to-all-start = ((f32[8,256,512]{2,1,0:T(8,128)}), f32[8,256,512]{2,1,0:T(8,128)}, u32[]{:S(2)}, u32[]{:S(2)}) async-start(f32[8,256,512]{2,1,0:T(8,128)} %select_select_fusion), calls=%async_computation | async-start | bytes 8388608 | tf_op jit(solution)/shard_map/all_to_all | solution.py:114
  74.2 90.5 %all-to-all-done = f32[8,256,512]{2,1,0:T(8,128)} async-done(((f32[8,256,512]{2,1,0:T(8,128)}), f32[8,256,512]{2,1,0:T(8,128)}, u32[]{:S(2)}, u32[]{:S(2)}) %all-to-all-start) | async-done | bytes 4194336 | tf_op jit(solution)/shard_map/all_to_all | solution.py:114
  164.6 5.3 %copy.60 = f32[8,256,512]{1,2,0:T(8,128)} copy(f32[8,256,512]{2,1,0:T(8,128)} %all-to-all-done) | data formatting | bytes 8388608 | tf_op jit(solution)/shard_map/all_to_all | solution.py:114
  170.0 4.6 %bitcast_multiply_fusion = f32[256,8,512]{0,2,1:T(8,128)} fusion(f32[8,256,512]{1,2,0:T(8,128)} %copy.60, f32[256,8]{0,1:T(8,128)S(1)} %bitcast.100), kind=kLoop, calls=%fused_computation.20 | loop fusion | flops 1048576 | bytes 8396800 | tf_op jit(solution)/shard_map/mul | solution.py:120
  174.6 5.6 %copy.77 = f32[256,4096]{1,0:T(8,128)} copy(f32[256,4096]{0,1:T(8,128)} %bitcast.91) | data formatting | bytes 8388608 | tf_op jit(solution)/shard_map/reshape | solution.py:120
  180.2 0.6 copy-done.2
  180.9 0.1 fusion.45
  181.0 0.1 copy.61
  181.1 0.1 copy.62
  181.2 0.1 copy.64
  181.3 0.1 copy.65
  181.4 0.1 copy.63
  181.5 0.1 copy.66
  181.6 0.7 dynamic-slice.1
  183.0 0.1 multiply_add_fusion
  183.1 0.1 broadcast_multiply_fusion
  183.2 4.8 %fusion.25 = f32[2,256,286]{2,0,1:T(2,128)S(1)} fusion(f32[2,31,1]{1,0,2:T(2,128)S(1)} %bitcast.111, s32[256,286]{1,0:T(8,128)S(1)} %iota_subtract_fusion), kind=kOutput, calls=%fused_computation.40 | convolution fusion | flops 56742400 | bytes 878840 | tf_op jit(solution)/shard_map/rqi,ki->krq/dot_general | solution.py:48
  188.0 4.2 %add_add_fusion = f32[4,2,256,1024]{3,2,0,1:T(8,128)} fusion(f32[4,2,1024]{2,0,1:T(4,128)S(1)} %get-tuple-element.32, f32[1024]{0:T(1024)S(1)} %multiply_add_fusion.1, f32[4,2,256]{2,0,1:T(4,128)S(1)} %get-tuple-element.36, f32[4,2,256]{2,0,1:T(4,128)S(1)} %get-tuple-element.37, f32[4,2,1024]{2,0,1:T(4,128)S(1)} %get-tuple-element.31, ...), kind=kLoop, calls=%fused_computation.7 | loop fusion | flops 10485760 | bytes 8482816 | tf_op jit(solution)/shard_map/add | solution.py:34
  192.2 8.9 %all-reduce.1 = f32[256,8]{0,1:T(8,128)S(1)} all-reduce(f32[256,8]{0,1:T(8,128)S(1)} %bitcast.101), channel_id=3, replica_groups=mesh['epoch'=4,'strip'=8] {'epoch'}, use_global_device_ids=true, to_apply=%region_6.7.clone | all-reduce | flops 2048 | bytes 16384
  201.1 0.1 copy.69
  201.2 0.3 div.32
  201.6 0.2 copy.81
  201.8 33.3 %reduce-scatter.2.cloned.1.call-done = f32[256,1024]{1,0:T(8,128)} async-done(((f32[256,4096]{1,0:T(8,128)}), f32[256,1024]{1,0:T(8,128)}) %reduce-scatter.2.cloned.1.call-update) | async-done | bytes 1048592 | tf_op jit(solution)/shard_map/reduce_scatter | solution.py:126
  235.1 1.4 div.34
  236.5 0.1 fusion.44
  236.6 3.1 collective-permute-start
  239.7 1.3 collective-permute-start.1
  241.0 0.6 collective-permute-done
  241.6 5.1 %collective-permute-done.1 = f32[256,15]{1,0:T(8,128)S(1)} collective-permute-done((f32[256,15]{1,0:T(8,128)S(1)}, f32[256,15]{1,0:T(8,128)S(1)}, u32[]{:S(2)}, u32[]{:S(2)}) %collective-permute-start.1) | collective-permute-done | bytes 15392 | tf_op jit(solution)/shard_map/ppermute | solution.py:19
  246.7 0.8 concatenate.9
  247.5 4.4 %collective-permute-start.2 = (f32[15,1054]{1,0:T(8,128)S(1)}, f32[15,1054]{1,0:T(8,128)S(1)}, u32[]{:S(2)}, u32[]{:S(2)}) collective-permute-start(f32[15,1054]{1,0:T(8,128)S(1)} %get-tuple-element.17), channel_id=1, source_target_pairs={{0,1},{1,2},{2,3},{3,4},{4,5},{5,6},{6,7},{8,9},{9,10},{10,11},{11... | collective-permute-start | bytes 189728 | tf_op jit(solution)/shard_map/ppermute | solution.py:18
  251.9 2.1 collective-permute-start.3
  254.1 1.0 fusion.27
  255.1 2.5 collective-permute-done.3
  257.6 3.7 %fusion.20 = f32[2,256,1054]{1,2,0:T(8,128)S(1)} fusion(f32[15,1054]{1,0:T(8,128)S(1)} %collective-permute-done.3, f32[256,1054]{1,0:T(8,128)S(1)} %concatenate.9, f32[15,1054]{1,0:T(8,128)S(1)} %collective-permute-done.2, f32[2,256,286]{2,0,1:T(2,128)S(1)} %fusion.25), kind=kOutput, calls=%fused_computation.35 | convolution fusion | flops 1852674816 | bytes 3950096 | tf_op jit(solution)/shard_map/krq,qc->krc/dot_general | solution.py:49
  261.3 0.3 fusion.41
  261.7 2.3 fusion.13
  263.9 0.1 fusion.42
  264.1 0.3 copy.72
  264.4 0.3 copy.73
  264.8 4.7 %fusion.8 = f32[4,256,1024]{2,1,0:T(8,128)S(1)} fusion(f32[4,2,256,1024]{3,2,0,1:T(8,128)} %add_add_fusion, f32[256,1024]{1,0:T(8,128)S(1)} %copy.73, f32[256,1024]{1,0:T(8,128)S(1)} %copy.72), kind=kLoop, calls=%fused_computation.15 | loop fusion | flops 3145728 | bytes 14680064 | tf_op jit(solution)/shard_map/add | solution.py:136
  269.5 0.5 slice_bitcast_fusion.5
  270.0 0.5 pad_maximum_fusion
  270.5 50.8 %all_to_all.16 = f32[4,1,256,1024]{3,2,1,0:T(8,128)} all-to-all(f32[4,1,256,1024]{3,2,1,0:T(8,128)S(1)} %pad_maximum_fusion), channel_id=1, replica_groups=mesh['epoch'=4,'strip'=8] {'epoch'}, dimensions={0} | all-to-all | bytes 8388608 | tf_op jit(solution)/shard_map/all_to_all | solution.py:138
  321.4 5.4 %copy.74 = f32[4,1,256,1024]{2,3,0,1:T(8,128)} copy(f32[4,1,256,1024]{3,2,1,0:T(8,128)} %all_to_all.16) | data formatting | bytes 8388608 | tf_op jit(solution)/shard_map/all_to_all | solution.py:138
  326.7 6.1 %bitcast_subtract_fusion = f32[1,256,4096]{1,2,0:T(8,128)} fusion(f32[4,1,256,1024]{2,3,0,1:T(8,128)} %copy.74, f32[1,256,4096]{1,2,0:T(8,128)} %bitcast.89), kind=kLoop, calls=%fused_computation.19 | loop fusion | flops 1048576 | bytes 12582912 | tf_op jit(solution)/shard_map/sub | solution.py:143
  332.8 5.6 %copy.75 = f32[1,256,4096]{2,1,0:T(8,128)} copy(f32[1,256,4096]{1,2,0:T(8,128)} %bitcast_subtract_fusion) | data formatting | bytes 8388608 | tf_op jit(solution)/shard_map/sub | solution.py:143
  (37 shorter events, 0.3 us)
Async XLA Ops:
  6.5 10.4 %copy-start = (f32[4,256,256]{2,1,0:T(8,128)S(1)}, f32[4,256,256]{2,1,0:T(8,128)}, u32[]{:S(2)}) copy-start(f32[4,256,256]{2,1,0:T(8,128)} %param.12) | copy-start | bytes 3145732
  9.9 59.2 %all-to-all-start.1 = ((f32[8,1,256]{2,1,0:T(1,128)}), f32[8,1,256]{2,1,0:T(1,128)S(1)}, u32[]{:S(2)}, u32[]{:S(2)}) async-start(f32[8,1,256]{2,1,0:T(1,128)} %copy.67), calls=%async_computation.1 | async-start | bytes 16384 | tf_op jit(solution)/shard_map/all_to_all | solution.py:115
  69.1 95.6 %all-to-all-start = ((f32[8,256,512]{2,1,0:T(8,128)}), f32[8,256,512]{2,1,0:T(8,128)}, u32[]{:S(2)}, u32[]{:S(2)}) async-start(f32[8,256,512]{2,1,0:T(8,128)} %select_select_fusion), calls=%async_computation | async-start | bytes 8388608 | tf_op jit(solution)/shard_map/all_to_all | solution.py:114
  74.2 160.9 %reduce-scatter.2.cloned.1.call-start = ((), (), s32[]{:S(2)}) async-start(), calls=%async_computation.4 | async-start | bytes 5242880 | tf_op jit(solution)/shard_map/reduce_scatter | solution.py:126
  180.2 0.7 copy-start.2
  180.2 1.4 copy-start.4
  180.2 2.8 copy-start.3
  236.6 5.0 %collective-permute-start = (f32[256,15]{1,0:T(8,128)S(1)}, f32[256,15]{1,0:T(8,128)S(1)}, u32[]{:S(2)}, u32[]{:S(2)}) collective-permute-start(f32[256,15]{1,0:T(8,128)S(1)} %get-tuple-element.20), channel_id=1, source_target_pairs={{0,8},{8,16},{16,24},{1,9},{9,17},{17,25},{2,10},{10,18},{18,26},{... | collective-permute-start | bytes 46088 | tf_op jit(solution)/shard_map/ppermute | solution.py:18
  239.7 7.0 %collective-permute-start.1 = (f32[256,15]{1,0:T(8,128)S(1)}, f32[256,15]{1,0:T(8,128)S(1)}, u32[]{:S(2)}, u32[]{:S(2)}) collective-permute-start(f32[256,15]{1,0:T(8,128)S(1)} %get-tuple-element.19), channel_id=1, source_target_pairs={{8,0},{16,8},{24,16},{9,1},{17,9},{25,17},{10,2},{18,10},{26,18},{... | collective-permute-start | bytes 46088 | tf_op jit(solution)/shard_map/ppermute | solution.py:19
  247.5 7.6 %collective-permute-start.2 = (f32[15,1054]{1,0:T(8,128)S(1)}, f32[15,1054]{1,0:T(8,128)S(1)}, u32[]{:S(2)}, u32[]{:S(2)}) collective-permute-start(f32[15,1054]{1,0:T(8,128)S(1)} %get-tuple-element.17), channel_id=1, source_target_pairs={{0,1},{1,2},{2,3},{3,4},{4,5},{5,6},{6,7},{8,9},{9,10},{10,11},{11... | collective-permute-start | bytes 189728 | tf_op jit(solution)/shard_map/ppermute | solution.py:18
  251.9 5.7 %collective-permute-start.3 = (f32[15,1054]{1,0:T(8,128)S(1)}, f32[15,1054]{1,0:T(8,128)S(1)}, u32[]{:S(2)}, u32[]{:S(2)}) collective-permute-start(f32[15,1054]{1,0:T(8,128)S(1)} %get-tuple-element.18), channel_id=1, source_target_pairs={{1,0},{2,1},{3,2},{4,3},{5,4},{6,5},{7,6},{9,8},{10,9},{11,10},{12... | collective-permute-start | bytes 189728 | tf_op jit(solution)/shard_map/ppermute | solution.py:19
  326.7 11.7 %copy-start.1 = (f32[4,256,256]{2,1,0:T(8,128)S(1)}, f32[4,256,256]{2,1,0:T(8,128)}, u32[]{:S(2)}) copy-start(f32[4,256,256]{2,1,0:T(8,128)} %param.12) | copy-start | bytes 3145732
Sparse Core Ops, SparseCore 0:
  180.3 54.6 reduce-scatter.1
